TPU v7x, 512 devices: a whole 4x8x8 slice. The times are simulated.
512 devices in a mesh: seq: 128 (over z_lo, x, y), head: 4 (over z_hi, core).
Axes of the slice: x: 4, y: 8, z: 8 (z_hi: 2, z_lo: 4; z = z_hi * 4 + z_lo), core: 2. Of those that a mesh axis runs over, the one named last changes fastest.
Arguments:
- queries: bfloat16 [16384, 2048], P('seq', 'head'), may hold values from -150 to 150
- keys: bfloat16 [16384, 1024], P('seq', 'head'), may hold values from -5 to 5
- values: bfloat16 [16384, 1024], P('seq', 'head'), may hold values from -5 to 5
- prefix_resid: bfloat16 [16384, 5376], P('seq', 'head'), may hold values from -6 to 6
- opt_queries: bfloat16 [128, 64, 2048], P('seq', None, 'head'), may hold values from -150 to 150
- opt_keys: bfloat16 [128, 64, 1024], P('seq', None, 'head'), may hold values from -5 to 5
- opt_values: bfloat16 [128, 64, 1024], P('seq', None, 'head'), may hold values from -5 to 5
- opt_resid: bfloat16 [128, 64, 5376], P('seq', None, 'head'), may hold values from -6 to 6
- out_weight: bfloat16 [2048, 5376], P('seq', 'head'), may hold values from -0.5347495 to 0.5347495
- norm_gain: float32 [5376], P('head'), may hold values from 0.1 to 1.9
- option_bounds: int32 [128, 2], P('seq'), may hold values from 0 to 64, as said below
Outputs:
- prefix_out: bfloat16 [16384, 5376], P('seq', 'head')
- option_out: bfloat16 [128, 64, 5376], P('seq', None, 'head')
- option_summary: float32 [128, 5376], P('seq', 'head')
Inputs may be any that keep to these rules, and one draw needn't show every extreme that they name: `option_bounds`: column 0 is an option's first answer position and column 1 its length, with 0 <= start < length; some option has length 64.
All inputs are finite; a program needn't handle non-finite values.
Results may differ from a plain program's by a relative error of at most 0.009.
Values may be sent and summed in bfloat16 or wider, within the bound.
A program may use at most 64 MiB of HBM per device.

v0:
```python
import jax
import jax.numpy as jnp
from jax import lax
from jax.sharding import PartitionSpec as P

D = 5376
HD = 128
WINDOW = 1024
OPT_LEN = 64


score_scale = 168.0 ** (-0.5)
epsilon = 1e-06


def passed_along(value, axis, steps):
    count = lax.axis_size(axis)
    initial, last = (max(0, -steps), min(count, count - steps))
    return lax.ppermute(value, axis, [(source, source + steps) for source in range(initial, last)])


def from_root(block, axis, owner):
    block = jnp.where(lax.axis_index(axis) == owner, block, jnp.zeros_like(block))
    return lax.psum(block, axis)


def attend(query_rows, key_rows, value_rows, allowed):
    row_count = query_rows.shape[0]
    kv_heads = key_rows.shape[1] // HD
    groups = query_rows.shape[1] // key_rows.shape[1]
    query_view = query_rows.reshape(row_count, kv_heads, groups, HD)
    key_view = key_rows.reshape(-1, kv_heads, HD)
    scores = (
        jnp.einsum("rkgd,lkd->kgrl", query_view, key_view, preferred_element_type=jnp.float32)
        * score_scale
    )
    scores = jnp.where(allowed[None, None], scores, -jnp.inf)
    row_max = jnp.max(scores, axis=-1, keepdims=True)
    weights = jnp.exp(scores - row_max)
    weights = (weights / jnp.sum(weights, axis=-1, keepdims=True)).astype(jnp.bfloat16)
    value_view = value_rows.reshape(-1, kv_heads, HD)
    attended = jnp.einsum("kgrl,lkd->rkgd", weights, value_view, preferred_element_type=jnp.float32)
    return attended.reshape(row_count, -1).astype(jnp.bfloat16)


def body(
    queries,
    keys,
    values,
    prefix_resid,
    opt_queries,
    opt_keys,
    opt_values,
    opt_resid,
    out_weight,
    norm_gain,
    option_bounds,
):
    local_rows = queries.shape[0]
    seq_count = lax.axis_size("seq")
    seq_index = lax.axis_index("seq")
    halo_count = WINDOW // local_rows
    earlier_keys = []
    earlier_values = []
    carried = (keys, values)
    for hop_index in range(halo_count):
        carried = passed_along((carried[0], carried[1]), "seq", 1)
        earlier_keys.insert(0, carried[0])
        earlier_values.insert(0, carried[1])
    window_keys = jnp.concatenate(earlier_keys + [keys], axis=0)
    window_values = jnp.concatenate(earlier_values + [values], axis=0)
    query_pos = seq_index * local_rows + jnp.arange(local_rows, dtype=jnp.int32)
    key_pos = (seq_index - halo_count) * local_rows + jnp.arange(
        window_keys.shape[0], dtype=jnp.int32
    )
    allowed = (
        (key_pos[None] <= query_pos[:, None])
        & (key_pos[None] > query_pos[:, None] - WINDOW)
        & (key_pos[None] >= 0)
    )
    prefix_attn = attend(queries, window_keys, window_values, allowed)
    final_keys, final_values = (
        from_root(window_keys[local_rows:], "seq", seq_count - 1),
        from_root(window_values[local_rows:], "seq", seq_count - 1),
    )
    joined_keys = jnp.concatenate([final_keys, opt_keys[0]], axis=0)
    joined_values = jnp.concatenate([final_values, opt_values[0]], axis=0)
    positions = jnp.arange(WINDOW + OPT_LEN, dtype=jnp.int32)
    option_pos = jnp.arange(OPT_LEN, dtype=jnp.int32)
    option_allowed = jnp.where(
        positions[None] < WINDOW,
        positions[None] > option_pos[:, None],
        positions[None] - WINDOW <= option_pos[:, None],
    )
    option_attn = attend(opt_queries[0], joined_keys, joined_values, option_allowed)
    stacked = jnp.concatenate([prefix_attn, option_attn], axis=0)
    weight_share = lax.all_gather(out_weight, "seq", axis=0, tiled=True)
    head_cols = stacked.shape[1]
    attn_whole = lax.all_gather(stacked, "head", axis=1, tiled=True)
    projected = jnp.zeros((stacked.shape[0], weight_share.shape[1]), jnp.float32)
    for group in range(lax.axis_size("head")):
        partial_value = jnp.dot(
            attn_whole[:, group * head_cols : (group + 1) * head_cols],
            weight_share[group * head_cols : (group + 1) * head_cols],
            preferred_element_type=jnp.float32,
        )
        projected = projected + lax.optimization_barrier(partial_value.astype(jnp.bfloat16)).astype(
            jnp.float32
        )
    squares = lax.psum(jnp.sum(projected * projected, axis=1), "head")
    normed = projected * lax.rsqrt(squares / D + epsilon)[:, None] * norm_gain[None, :]
    prefix_out = (prefix_resid.astype(jnp.float32) + normed[:local_rows]).astype(jnp.bfloat16)
    option_full = opt_resid[0].astype(jnp.float32) + normed[local_rows:]
    start_pos = option_bounds[0, 0]
    length = option_bounds[0, 1]
    inside = option_pos < length
    option_out = jnp.where(inside[:, None], option_full, 0.0).astype(jnp.bfloat16)
    chosen = inside & (option_pos >= start_pos)
    option_summary = jnp.sum(
        jnp.where(chosen[:, None], option_out.astype(jnp.float32), 0.0), axis=0
    ) / (length - start_pos).astype(jnp.float32)
    return (prefix_out, option_out[None], option_summary[None])


def solution(mesh):
    return jax.shard_map(
        body,
        mesh=mesh,
        in_specs=(
            P("seq", "head"),
            P("seq", "head"),
            P("seq", "head"),
            P("seq", "head"),
            P("seq", None, "head"),
            P("seq", None, "head"),
            P("seq", None, "head"),
            P("seq", None, "head"),
            P("seq", "head"),
            P("head"),
            P("seq", None),
        ),
        out_specs=(P("seq", "head"), P("seq", None, "head"), P("seq", "head")),
        check_vma=False,
    )
```

profile of v0, /device:TPU:1, one launch (start us, length us, event | category | flops | bytes accessed | tf_op | source)
XLA Modules:
  0.0 2241.2 jit_solution(12938936736685108512)
XLA Ops:
  7.2 0.9 copy.21
  8.2 4.0 collective-permute-start
  12.2 1.0 copy.23
  13.2 3.2 collective-permute-start.8
  16.4 3.2 collective-permute-start.1
  19.6 4.4 collective-permute-start.9
  24.0 2.3 collective-permute-start.2
  26.4 2.9 collective-permute-start.10
  29.3 3.3 collective-permute-start.3
  32.6 2.9 collective-permute-start.11
  35.5 3.3 collective-permute-start.4
  38.8 3.2 collective-permute-start.12
  42.0 3.8 collective-permute-start.5
  45.8 2.4 collective-permute-start.13
  48.3 3.8 collective-permute-start.6
  52.0 2.5 collective-permute-start.14
  54.6 3.7 collective-permute-start.7
  58.2 4.3 collective-permute-start.15
  62.9 1.4 collective-permute-done.15
  64.6 0.1 broadcast_select_fusion
  64.7 1.0 copy.29
  65.7 1.0 copy.32
  66.8 0.7 all-gather.2.cloned.1.call-update
  67.7 0.9 copy.20
  68.6 0.6 fusion.58
  70.5 1.3 compare_and_fusion
  71.9 0.1 fusion.24
  71.9 0.9 and_and_fusion
  72.8 1.0 fusion.62
  73.8 1.3 fusion.15
  75.1 1354.7 %all-reduce.3.cloned.1.call-done = (bf16[1024,2,128]{2,0,1:T(8,128)(2,1)}, bf16[1024,2,128]{2,0,1:T(8,128)(2,1)}) async-done(((bf16[1024,2,128]{2,0,1:T(8,128)(2,1)}, bf16[1024,2,128]{2,0,1:T(8,128)(2,1)}), (bf16[1024,2,128]{2,0,1:T(8,128)(2,1)}, bf16[1024,2,128]{2,0,1:T(8,128)(2,1)})) %all-reduce.3.cloned.1.call-update) | async-done | bytes 1048592 | tf_op jit(solution)/shard_map/psum | solution.py:24
  1429.7 1.7 fusion.59
  1431.5 0.4 fusion.16
  1431.8 0.1 copy.45
  1432.0 106.8 %all_gather.6 = bf16[192,2048]{0,1:T(8,128)(2,1)S(1)} all-gather(bf16[192,512]{0,1:T(8,128)(2,1)S(1)} %pad_maximum_fusion), channel_id=1, replica_groups=mesh['seq'=128,'head'=4] {'head'}, dimensions={1}, use_global_device_ids=true | all-gather | bytes 983040 | tf_op jit(solution)/shard_map/all_gather | solution.py:99
  1538.9 579.6 %all-gather.2.cloned.1.call-done = bf16[2048,1344]{1,0:T(8,128)(2,1)} async-done(((bf16[16,1344]{1,0:T(8,128)(2,1)}), bf16[2048,1344]{1,0:T(8,128)(2,1)}) %all-gather.2.cloned.1.call-update) | async-done | bytes 5505040 | tf_op jit(solution)/shard_map/all_gather | solution.py:97
  2118.5 1.9 convolution_convert_fusion.3
  2120.4 1.9 convolution_convert_fusion.2
  2122.3 1.9 convolution_convert_fusion.1
  2124.1 1.9 convolution_convert_fusion
  2126.0 0.4 multiply_reduce_fusion
  2126.4 104.6 %psum.23 = f32[192]{0:T(256)S(1)} all-reduce(f32[192]{0:T(256)S(1)} %multiply_reduce_fusion), channel_id=1, replica_groups=mesh['seq'=128,'head'=4] {'head'}, use_global_device_ids=true, to_apply=%region_7.8 | all-reduce | flops 192 | bytes 1536 | tf_op jit(solution)/shard_map/psum | solution.py:110
  2231.0 0.3 multiply_multiply_fusion
  2231.3 0.7 copy-done
  2232.0 0.1 fusion.17
  2232.1 0.9 copy.37
  2233.0 0.8 select_reduce_fusion
  2233.8 0.6 div.46
  (69 shorter events, 0.9 us)
Async XLA Ops:
  7.2 1422.6 %all-reduce.3.cloned.1.call-start = ((), (), s32[]{:S(2)}) async-start(), calls=%async_computation.1 | async-start | bytes 2097152 | tf_op jit(solution)/shard_map/psum | solution.py:24
  8.2 8.2 collective-permute-start
  13.2 6.4 collective-permute-start.8
  16.4 7.6 collective-permute-start.1
  19.6 6.8 collective-permute-start.9
  24.0 5.3 collective-permute-start.2
  26.4 6.2 collective-permute-start.10
  29.3 6.2 collective-permute-start.3
  32.6 6.2 collective-permute-start.11
  35.5 6.5 collective-permute-start.4
  38.8 7.0 collective-permute-start.12
  42.0 6.2 collective-permute-start.5
  45.8 6.2 collective-permute-start.13
  48.3 6.3 collective-permute-start.6
  52.0 6.2 collective-permute-start.14
  54.6 8.0 collective-permute-start.7
  58.2 6.0 collective-permute-start.15
  65.7 1.8 copy-start.3
  65.7 1.9 copy-start.5
  65.7 1.9 copy-start.4
  65.7 1.9 copy-start.6
  65.7 2.0 copy-start.1
  66.7 1.9 copy-start.8
  66.7 2051.8 %all-gather.2.cloned.1.call-start = ((), (), s32[]{:S(2)}) async-start(), calls=%async_computation | async-start | bytes 5812224 | tf_op jit(solution)/shard_map/all_gather | solution.py:97
  1429.7 1.7 copy-start.9
  2126.0 105.0 %copy-start.7 = (f32[1344]{0:T(1024)S(1)}, f32[1344]{0:T(1024)}, u32[]{:S(2)}) copy-start(f32[1344]{0:T(1024)} %param.20) | copy-start | bytes 16132
  2231.0 1.0 copy-start
  2232.0 1.0 copy-start.2
Sparse Core Ops, SparseCore 0:
  66.9 1362.8 all-reduce.2
  1431.8 686.6 all-gather.1
where the time goes:
time: 2240 us
  waiting for transfers between devices  1940 us (87%)
  blocking collectives  211 us (9%)
  starting transfers between devices  53.2 us (2%)
    psum x1, waiting for transfers between devices, from_root(): return lax.psum(block, axis)  1350 us
    all_gather x1, waiting for transfers between devices, body(): weight_share = lax.all_gather(out_weight, 'seq', axis=0, tiled=True)  580 us
    all_gather x1, blocking collectives, body(): attn_whole = lax.all_gather(stacked, 'head', axis=1, tiled=True)  107 us
    psum x1, blocking collectives, body(): squares = lax.psum(jnp.sum(projected * projected, axis=1), 'head')  105 us
    ppermute x16, starting transfers between devices, passed_along(): lax.ppermute(value, axis, [(source, source + steps) for source in range(i...  53.1 us
  transfers between devices with their start and end apart: 18, of which 3 were waited for; matrix products, arithmetic and copies ran while one was open for 0% of the time, Pallas kernels for 0%

commit v1 on v0

v1 whole, which is shorter than its diff:
```python
import jax
import jax.numpy as jnp
from jax import lax
from jax.experimental import pallas as pl
from jax.experimental.pallas import tpu as pltpu
from jax.sharding import PartitionSpec as P

D = 5376
HD = 128
WINDOW = 1024
TOK = 128
OPT = 64
COLS = 1344
NY = 8
ROWS = TOK + OPT
MESH = pl.DeviceIdType.MESH

score_scale = 168.0 ** (-0.5)
epsilon = 1e-06
exp2_scale = score_scale * 1.4426950408889634

WYP, WYM = 0, 4
UP, DOWN = 8, 16
TREE, LP, LM = 24, 25, 30
WZ, XL, XR, HL, HR = 34, 38, 42, 46, 50
HEADS, SQ = 54, 60
N_RECV = 64
N_SEND = 96


def softmax_dot(scores, value_rows):
    top = jnp.max(scores, axis=1, keepdims=True)
    weights = jnp.exp2((scores - top) * exp2_scale)
    total = jnp.sum(weights, axis=1, keepdims=True)
    out = jnp.dot(weights.astype(jnp.bfloat16), value_rows, preferred_element_type=jnp.float32)
    return out / total


def score_dot(query_rows, key_rows):
    return lax.dot_general(
        query_rows, key_rows, (((1,), (1,)), ((), ())), preferred_element_type=jnp.float32
    )


def kernel(
    q_in, k_in, v_in, res_in, oq_in, ok_in, ov_in, ores_in, w_in, gain_in, bounds,
    pout, oout, osum,
    q, oq, ok, ov, res, ores, gain, kv, lkv, wbuf, abuf, proj, ssq,
    local_sem, send_sem, recv_sem,
):
    seq = lax.axis_index("seq")
    head = lax.axis_index("head")
    z = lax.div(seq, 32)
    x = lax.rem(lax.div(seq, 8), 4)
    y = lax.rem(seq, 8)
    zhi = lax.div(head, 2)
    core = lax.rem(head, 2)
    group = z * 4 + x

    def at(zz, xx, yy):
        return ((zz * 4 + xx) * 8 + yy, head)

    up_y = at(z, x, lax.rem(y + 1, 8))
    down_y = at(z, x, lax.rem(y + 7, 8))
    up_x = at(z, lax.rem(x + 1, 4), y)
    down_x = at(z, lax.rem(x + 3, 4), y)
    up_z = at(lax.rem(z + 1, 4), x, y)
    down_z = at(lax.rem(z + 3, 4), x, y)
    next_line = (lax.rem(seq + 8, 128), head)
    prev_line = (lax.rem(seq + 120, 128), head)
    h_sib = zhi * 2 + 1 - core
    h_far = (1 - zhi) * 2 + core
    h_farsib = (1 - zhi) * 2 + 1 - core
    sib = (seq, h_sib)
    far = (seq, h_far)
    farsib = (seq, h_farsib)

    local = []

    def load(src, dst, pred=None):
        copy = pltpu.make_async_copy(src, dst, local_sem.at[len(local)])
        local.append(copy)
        if pred is None:
            copy.start()
        else:
            pl.when(pred)(lambda: copy.start())
        return copy

    def rows16(g, yy):
        return wbuf.at[pl.ds(pl.multiple_of(g * 128 + yy * 16, 16), 16), :]

    def rows128(g):
        return wbuf.at[pl.ds(pl.multiple_of(g * 128, 128), 128), :]

    def rows64(g, half):
        return wbuf.at[pl.ds(pl.multiple_of(g * 128 + half * 64, 64), 64), :]

    is_source = (z == 3) & (x == 3)
    first = [
        load(k_in, kv.at[8, :, pl.ds(0, 256)]),
        load(v_in, kv.at[8, :, pl.ds(256, 256)]),
        load(w_in, rows16(group, y)),
    ]
    source_loads = [
        load(k_in, lkv.at[y, :, pl.ds(0, 256)], is_source),
        load(v_in, lkv.at[y, :, pl.ds(256, 256)], is_source),
    ]
    later = [
        load(q_in, q), load(oq_in, oq), load(ok_in, ok), load(ov_in, ov),
        load(res_in, res), load(ores_in, ores), load(gain_in, gain),
    ]

    barrier = pltpu.get_barrier_semaphore()
    partners = [up_y, down_y, up_x, down_x, up_z, down_z, next_line, prev_line, sib, far, farsib]
    for partner in partners:
        pl.semaphore_signal(barrier, inc=1, device_id=partner, device_id_type=MESH)
    for copy in first:
        copy.wait()

    @pl.when(is_source)
    def _():
        for copy in source_loads:
            copy.wait()

    pl.semaphore_wait(barrier, len(partners))

    sent = []

    def send(src, dst, recv, device, pred=None):
        copy = pltpu.make_async_remote_copy(
            src_ref=src, dst_ref=dst, send_sem=send_sem.at[len(sent)],
            recv_sem=recv_sem.at[recv], device_id=device, device_id_type=MESH,
        )
        sent.append((copy, pred))
        if pred is None:
            copy.start()
        else:
            pl.when(pred)(lambda: copy.start())

    def arrived(ref, recv, pred=None):
        copy = pltpu.make_async_remote_copy(
            src_ref=ref, dst_ref=ref, send_sem=send_sem.at[0],
            recv_sem=recv_sem.at[recv], device_id=sib, device_id_type=MESH,
        )
        if pred is None:
            copy.wait_recv()
        else:
            pl.when(pred)(lambda: copy.wait_recv())

    def mod8(value):
        return lax.rem(value + 8, 8)

    def wy_up(k):
        piece = rows16(group, mod8(y - k))
        if k:
            arrived(piece, WYP + k - 1)
        if k < 4:
            send(piece, piece, WYP + k, up_y)

    def wy_down(k):
        piece = rows16(group, lax.rem(y + k, 8))
        if k:
            arrived(piece, WYM + k - 1)
        if k < 3:
            send(piece, piece, WYM + k, down_y)

    def kv_up(k):
        if k:
            arrived(kv.at[8 - k], UP + k, y >= k)
        if k < 7:
            send(kv.at[8 - k], kv.at[7 - k], UP + k + 1, up_y, (y >= k) & (y < 7))

    def kv_down(m):
        arrived(kv.at[m], DOWN + m, y <= 7 - m)
        if m < 7:
            send(kv.at[m], kv.at[m + 1], DOWN + m + 1, down_y, (y <= 7 - m) & (y > 0))

    depth = lax.select(x == 3, 0, lax.select(x == 1, 2, 1)) + 3 - z

    def tree_sends(pred):
        piece = lkv.at[y]
        send(piece, piece, TREE, up_x, pred & (z == 3) & ((x == 3) | (x == 0)))
        send(piece, piece, TREE, down_x, pred & (z == 3) & (x == 3))
        send(piece, piece, TREE, down_z, pred & (z > 0))

    def tree(k):
        here = depth == k
        if k:
            arrived(lkv.at[y], TREE, here)
        tree_sends(here)

    def l_up(k):
        piece = lkv.at[mod8(y - k)]
        if k:
            arrived(piece, LP + k)
        if k < 4:
            send(piece, piece, LP + k + 1, up_y)

    def l_down(k):
        piece = lkv.at[lax.rem(y + k, 8)]
        if k:
            arrived(piece, LM + k)
        if k < 3:
            send(piece, piece, LM + k + 1, down_y)

    zhalf = lax.div(z, 2)
    order = [
        z,
        z - 1 + 2 * (1 - lax.div(z + 3, 4)),
        2 + zhalf * (1 - 2 * lax.rem(z, 2)),
        3 * (1 - zhalf),
    ]

    def z_event(i):
        plane = order[i]
        piece = rows128(plane * 4 + x)
        if i:
            arrived(piece, WZ + plane)
        send(piece, piece, WZ + plane, up_z, (plane <= z) & (z < 3))
        send(piece, piece, WZ + plane, down_z, (plane >= z) & (z > 0))
        send(piece, piece, XL + i, up_x)
        send(piece, piece, XR + i, down_x)

    def x_full(i):
        left = order[i] * 4 + lax.rem(x + 3, 4)
        right = order[i] * 4 + lax.rem(x + 1, 4)
        arrived(rows128(left), XL + i)
        send(rows64(left, 0), rows64(left, 0), HL + i, up_x)
        arrived(rows128(right), XR + i)
        send(rows64(right, 1), rows64(right, 1), HR + i, down_x)

    def x_half(i):
        across = order[i] * 4 + lax.rem(x + 2, 4)
        arrived(rows64(across, 0), HL + i)
        arrived(rows64(across, 1), HR + i)

    def prefix_pair(i):
        keys = kv[:, :, i * HD:(i + 1) * HD].reshape(9 * TOK, HD)
        vals = kv[:, :, 256 + i * HD:256 + (i + 1) * HD].reshape(9 * TOK, HD)
        for half in range(2):
            c = (2 * i + half) * HD
            scores = score_dot(q[:, c:c + HD], keys)
            row = lax.broadcasted_iota(jnp.int32, scores.shape, 0)
            col = lax.broadcasted_iota(jnp.int32, scores.shape, 1)
            allowed = (col > row) & (col <= row + WINDOW) & (col >= (8 - seq) * TOK)
            scores = jnp.where(allowed, scores, -jnp.inf)
            abuf[head, 0:TOK, c:c + HD] = softmax_dot(scores, vals).astype(jnp.bfloat16)

    def option_pair(i):
        keys = lkv[:, :, i * HD:(i + 1) * HD].reshape(WINDOW, HD)
        vals = lkv[:, :, 256 + i * HD:256 + (i + 1) * HD].reshape(WINDOW, HD)
        own_keys = ok[:, i * HD:(i + 1) * HD]
        own_vals = ov[:, i * HD:(i + 1) * HD]
        for half in range(2):
            c = (2 * i + half) * HD
            query = oq[:, c:c + HD]
            shared = score_dot(query, keys)
            own = score_dot(query, own_keys)
            row = lax.broadcasted_iota(jnp.int32, shared.shape, 0)
            col = lax.broadcasted_iota(jnp.int32, shared.shape, 1)
            shared = jnp.where(col > row, shared, -jnp.inf)
            row = lax.broadcasted_iota(jnp.int32, own.shape, 0)
            col = lax.broadcasted_iota(jnp.int32, own.shape, 1)
            own = jnp.where(col <= row, own, -jnp.inf)
            top = jnp.maximum(
                jnp.max(shared, axis=1, keepdims=True), jnp.max(own, axis=1, keepdims=True)
            )
            ws = jnp.exp2((shared - top) * exp2_scale)
            wo = jnp.exp2((own - top) * exp2_scale)
            total = jnp.sum(ws, axis=1, keepdims=True) + jnp.sum(wo, axis=1, keepdims=True)
            out = jnp.dot(ws.astype(jnp.bfloat16), vals, preferred_element_type=jnp.float32)
            out = out + jnp.dot(
                wo.astype(jnp.bfloat16), own_vals, preferred_element_type=jnp.float32
            )
            abuf[head, TOK:ROWS, c:c + HD] = (out / total).astype(jnp.bfloat16)

    def exchange_send(part):
        rows = pl.ds(0, TOK) if part == 0 else pl.ds(TOK, OPT)
        piece = abuf.at[head, rows, :]
        send(piece, piece, HEADS + 3 * part, far_first[0])
        send(piece, piece, HEADS + 3 * part + 1, far_first[1])

    far_first = (far, sib)

    def exchange_forward(part):
        rows = pl.ds(0, TOK) if part == 0 else pl.ds(TOK, OPT)
        piece = abuf.at[h_far, rows, :]
        arrived(piece, HEADS + 3 * part)
        send(piece, piece, HEADS + 3 * part + 2, sib)

    def exchange_rest(part):
        rows = pl.ds(0, TOK) if part == 0 else pl.ds(TOK, OPT)
        arrived(abuf.at[h_sib, rows, :], HEADS + 3 * part + 1)
        arrived(abuf.at[h_farsib, rows, :], HEADS + 3 * part + 2)

    def project(i):
        plane = order[i]
        part = jnp.dot(
            abuf[plane], wbuf[pl.ds(pl.multiple_of(plane * 512, 512), 512), :],
            preferred_element_type=jnp.float32,
        )
        if i == 0:
            proj[...] = part
        else:
            proj[...] += part

    wy_up(0)
    wy_down(0)
    kv_up(0)
    send(kv.at[8], kv.at[0], DOWN, next_line)
    tree(0)
    for k in range(1, 8):
        kv_down(k - 1)
        kv_up(k)
        if k <= 4:
            wy_up(k)
        if k <= 3:
            wy_down(k)
        if k == 4:
            z_event(0)
        if k <= 5:
            tree(k)
        if k == 6:
            z_event(1)
        if k == 7:
            x_full(0)
    kv_down(7)
    l_up(0)
    l_down(0)
    for copy in later[:4]:
        copy.wait()
    prefix_pair(0)
    l_up(1)
    l_down(1)
    z_event(2)
    prefix_pair(1)
    exchange_send(0)
    l_up(2)
    l_down(2)
    x_full(1)
    l_up(3)
    l_down(3)
    exchange_forward(0)
    l_up(4)
    option_pair(0)
    option_pair(1)
    exchange_send(1)
    z_event(3)
    x_full(2)
    exchange_rest(0)
    exchange_forward(1)
    exchange_rest(1)
    x_half(0)
    project(0)
    x_full(3)
    for i in range(1, 4):
        x_half(i)
        project(i)

    square = jnp.sum(proj[...] * proj[...], axis=1, keepdims=True)
    diag = (
        lax.broadcasted_iota(jnp.int32, (128, 128), 0)
        == lax.broadcasted_iota(jnp.int32, (128, 128), 1)
    )
    row0 = jnp.sum(jnp.where(diag, square[0:128], 0.0), axis=0, keepdims=True)
    row1 = jnp.sum(jnp.where(diag[0:64], square[128:192], 0.0), axis=0, keepdims=True)
    ssq[head] = jnp.concatenate([row0, row1, jnp.zeros((6, 128), jnp.float32)], axis=0)
    mine = ssq.at[head]
    send(mine, mine, SQ, far)
    send(mine, mine, SQ + 1, farsib)
    send(mine, mine, SQ + 2, sib)
    for copy in later[4:]:
        copy.wait()
    arrived(ssq.at[h_sib], SQ + 2)
    arrived(ssq.at[h_far], SQ)
    arrived(ssq.at[h_farsib], SQ + 1)
    total = ssq[0] + ssq[1] + ssq[2] + ssq[3]
    col0 = jnp.sum(jnp.where(diag, total[0:1], 0.0), axis=1, keepdims=True)
    col1 = jnp.sum(jnp.where(diag[0:64], total[1:2], 0.0), axis=1, keepdims=True)
    inv0 = lax.rsqrt(col0 / D + epsilon)
    inv1 = lax.rsqrt(col1 / D + epsilon)
    pout[...] = (
        res[...].astype(jnp.float32) + proj[0:TOK, :] * inv0 * gain[...]
    ).astype(jnp.bfloat16)
    full = ores[...].astype(jnp.float32) + proj[TOK:ROWS, :] * inv1 * gain[...]
    start = bounds[0, 0]
    length = bounds[0, 1]
    pos = lax.broadcasted_iota(jnp.int32, (OPT, COLS), 0)
    inside = pos < length
    out = jnp.where(inside, full, 0.0).astype(jnp.bfloat16)
    oout[...] = out
    chosen = inside & (pos >= start)
    picked = jnp.where(chosen, out.astype(jnp.float32), 0.0)
    count = jnp.broadcast_to((length - start).astype(jnp.float32), (1, COLS))
    osum[...] = jnp.sum(picked, axis=0, keepdims=True) / count

    for copy, pred in sent:
        if pred is None:
            copy.wait_send()
        else:
            pl.when(pred)(lambda copy=copy: copy.wait_send())


def fused(*args):
    bf, f32 = jnp.bfloat16, jnp.float32
    anywhere = pl.BlockSpec(memory_space=pl.ANY)
    vmem = pl.BlockSpec(memory_space=pltpu.VMEM)
    return pl.pallas_call(
        kernel,
        out_shape=(
            jax.ShapeDtypeStruct((TOK, COLS), bf),
            jax.ShapeDtypeStruct((OPT, COLS), bf),
            jax.ShapeDtypeStruct((1, COLS), f32),
        ),
        in_specs=[anywhere] * 10 + [pl.BlockSpec(memory_space=pltpu.SMEM)],
        out_specs=(vmem, vmem, vmem),
        scratch_shapes=[
            pltpu.VMEM((TOK, 512), bf),
            pltpu.VMEM((OPT, 512), bf),
            pltpu.VMEM((OPT, 256), bf),
            pltpu.VMEM((OPT, 256), bf),
            pltpu.VMEM((TOK, COLS), bf),
            pltpu.VMEM((OPT, COLS), bf),
            pltpu.VMEM((1, COLS), f32),
            pltpu.VMEM((9, TOK, 512), bf),
            pltpu.VMEM((8, TOK, 512), bf),
            pltpu.VMEM((2048, COLS), bf),
            pltpu.VMEM((4, ROWS, 512), bf),
            pltpu.VMEM((ROWS, COLS), f32),
            pltpu.VMEM((4, 8, 128), f32),
            pltpu.SemaphoreType.DMA((16,)),
            pltpu.SemaphoreType.DMA((N_SEND,)),
            pltpu.SemaphoreType.DMA((N_RECV,)),
        ],
        compiler_params=pltpu.CompilerParams(
            collective_id=0, has_side_effects=True, vmem_limit_bytes=48 * 1024 * 1024
        ),
    )(*args)


def body(
    queries, keys, values, prefix_resid, opt_queries, opt_keys, opt_values, opt_resid,
    out_weight, norm_gain, option_bounds,
):
    prefix_out, option_out, option_summary = fused(
        queries, keys, values, prefix_resid, opt_queries[0], opt_keys[0], opt_values[0],
        opt_resid[0], out_weight, norm_gain[None, :], option_bounds,
    )
    return prefix_out, option_out[None], option_summary[None, 0]


def solution(mesh):
    return jax.shard_map(
        body,
        mesh=mesh,
        in_specs=(
            P("seq", "head"),
            P("seq", "head"),
            P("seq", "head"),
            P("seq", "head"),
            P("seq", None, "head"),
            P("seq", None, "head"),
            P("seq", None, "head"),
            P("seq", None, "head"),
            P("seq", "head"),
            P("head"),
            P("seq", None),
        ),
        out_specs=(P("seq", "head"), P("seq", None, "head"), P("seq", "head")),
        check_vma=False,
    )
```

time: 2240 us -> 106 us (0.05)
  the two profiles are of different devices: /device:TPU:1 before, /device:TPU:59 now
where the time goes in v1:
time: 106 us; the launch traced here: 105 us
  Pallas kernels  100 us (94%)
  local copies, waits for them, and re-layouts  4.22 us (4%)
    pallas_call x1, Pallas kernels, fused(): pl.pallas_call(kernel, out_shape=(jax.ShapeDtypeStruct((TOK, COLS), bf),...  100 us
    unnamed x22, local copies, waits for them, and re-layouts  3.52 us

profile of v1, /device:TPU:59, one launch (start us, length us, event | category | flops | bytes accessed | tf_op | source)
XLA Modules:
  0.0 105.4 jit_solution(4192431435004962608)
XLA Ops:
  0.6 0.7 broadcast_in_dim.6.gain_in
  1.3 0.0 copy-start
  1.3 0.0 copy-start.1
  1.3 0.0 copy-start.2
  1.3 0.0 copy-start.3
  1.4 0.0 copy-start.4
  1.4 0.0 copy-start.5
  1.4 0.0 copy-start.6
  1.4 0.0 copy-start.7
  1.4 0.0 copy-start.8
  1.4 1.3 %copy.14.res_in = bf16[128,1344]{1,0:T(8,128)(2,1)S(1)} copy(bf16[128,1344]{0,1:T(8,128)(2,1)} %param.14) | data formatting | bytes 688128 | tf_op args[3]
  2.7 0.0 copy-done
  2.7 0.0 copy-done.1
  2.7 0.0 copy-done.2
  2.7 0.0 copy-done.3
  2.8 0.0 copy-done.4
  2.8 0.0 copy-done.5
  2.8 0.0 copy-done.6
  2.8 0.0 copy-done.7
  2.8 0.0 copy-done.8
  2.8 100.4 %shard_map.130 = (bf16[128,1344]{1,0:T(8,128)(2,1)S(1)}, bf16[64,1344]{1,0:T(8,128)(2,1)S(1)}, f32[1,1344]{1,0:T(1,128)S(1)}) custom-call(bf16[128,512]{1,0:T(8,128)(2,1)S(1)} %copy-done.1, bf16[128,256]{1,0:T(8,128)(2,1)S(1)} %copy-done.2, bf16[128,256]{1,0:T(8,128)(2,1)S(1)} %copy-done.3, bf16[128,1344]{1,0:T(8,128)(2,1)S(1)} %copy.14.res_in, ...), custom_call_target="tpu_custom_call" | custom-call | tf_op jit(solution)/shard_map/pallas_call | solution.py:408
  103.3 0.9 copy.15
  104.2 0.7 copy.18
  104.8 0.6 copy.19
Async XLA Ops:
  1.3 1.4 %copy-start = (bf16[1,64,1344]{2,1,0:T(8,128)(2,1)S(1)}, bf16[1,64,1344]{2,1,0:T(8,128)(2,1)}, u32[]{:S(2)}) copy-start(bf16[1,64,1344]{2,1,0:T(8,128)(2,1)} %param.18) | copy-start | bytes 516100
  1.3 1.4 %copy-start.1 = (bf16[128,512]{1,0:T(8,128)(2,1)S(1)}, bf16[128,512]{1,0:T(8,128)(2,1)}, u32[]{:S(2)}) copy-start(bf16[128,512]{1,0:T(8,128)(2,1)} %q_in.1) | copy-start | bytes 393220
  1.3 1.4 %copy-start.2 = (bf16[128,256]{1,0:T(8,128)(2,1)S(1)}, bf16[128,256]{1,0:T(8,128)(2,1)}, u32[]{:S(2)}) copy-start(bf16[128,256]{1,0:T(8,128)(2,1)} %k_in.1) | copy-start | bytes 196612
  1.3 1.4 %copy-start.3 = (bf16[128,256]{1,0:T(8,128)(2,1)S(1)}, bf16[128,256]{1,0:T(8,128)(2,1)}, u32[]{:S(2)}) copy-start(bf16[128,256]{1,0:T(8,128)(2,1)} %v_in.1) | copy-start | bytes 196612
  1.4 1.4 %copy-start.4 = (bf16[1,64,512]{2,1,0:T(8,128)(2,1)S(1)}, bf16[1,64,512]{2,1,0:T(8,128)(2,1)}, u32[]{:S(2)}) copy-start(bf16[1,64,512]{2,1,0:T(8,128)(2,1)} %param.15) | copy-start | bytes 196612
  1.4 1.4 %copy-start.5 = (bf16[16,1344]{1,0:T(8,128)(2,1)S(1)}, bf16[16,1344]{1,0:T(8,128)(2,1)}, u32[]{:S(2)}) copy-start(bf16[16,1344]{1,0:T(8,128)(2,1)} %w_in.1) | copy-start | bytes 129028
  1.4 1.4 %copy-start.6 = (bf16[1,64,256]{2,1,0:T(8,128)(2,1)S(1)}, bf16[1,64,256]{2,1,0:T(8,128)(2,1)}, u32[]{:S(2)}) copy-start(bf16[1,64,256]{2,1,0:T(8,128)(2,1)} %param.16) | copy-start | bytes 98308
  1.4 1.4 %copy-start.7 = (bf16[1,64,256]{2,1,0:T(8,128)(2,1)S(1)}, bf16[1,64,256]{2,1,0:T(8,128)(2,1)}, u32[]{:S(2)}) copy-start(bf16[1,64,256]{2,1,0:T(8,128)(2,1)} %param.17) | copy-start | bytes 98308
  1.4 1.4 %copy-start.8 = (s32[1,2]{1,0:T(1,128)S(1)}, s32[1,2]{1,0:T(1,128)}, u32[]{:S(2)}) copy-start(s32[1,2]{1,0:T(1,128)} %bounds.1) | copy-start | bytes 28

commit v2 on v1

v2 whole, which is shorter than its diff:
```python
import jax
import jax.numpy as jnp
from jax import lax
from jax.experimental import pallas as pl
from jax.experimental.pallas import tpu as pltpu
from jax.sharding import PartitionSpec as P

D = 5376
HD = 128
WINDOW = 1024
TOK = 128
OPT = 64
COLS = 1344
NY = 8
ROWS = TOK + OPT
MESH = pl.DeviceIdType.MESH

score_scale = 168.0 ** (-0.5)
epsilon = 1e-06
exp2_scale = score_scale * 1.4426950408889634

N_RECV = 128
N_SEND = 224


def softmax_dot(scores, value_rows):
    top = jnp.max(scores, axis=1, keepdims=True)
    weights = jnp.exp2((scores - top) * exp2_scale)
    total = jnp.sum(weights, axis=1, keepdims=True)
    out = jnp.dot(weights.astype(jnp.bfloat16), value_rows, preferred_element_type=jnp.float32)
    return out / total


def score_dot(query_rows, key_rows):
    return lax.dot_general(
        query_rows, key_rows, (((1,), (1,)), ((), ())), preferred_element_type=jnp.float32
    )


def kernel(
    q_in, k_in, v_in, res_in, oq_in, ok_in, ov_in, ores_in, w_in, gain_in, bounds,
    pout, oout, osum,
    q, oq, ok, ov, rest, res, ores, gain, kv, lkv, wbuf, abuf, relay, proj, ssq,
    local_sem, send_sem, recv_sem,
):
    seq = lax.axis_index("seq")
    head = lax.axis_index("head")
    z = lax.div(seq, 32)
    x = lax.rem(lax.div(seq, 8), 4)
    y = lax.rem(seq, 8)
    zhi = lax.div(head, 2)
    core = lax.rem(head, 2)
    group = z * 4 + x

    def at(zz, xx, yy):
        return ((zz * 4 + xx) * 8 + yy, head)

    up_y = at(z, x, lax.rem(y + 1, 8))
    down_y = at(z, x, lax.rem(y + 7, 8))
    up_y2 = at(z, x, lax.rem(y + 2, 8))
    down_y2 = at(z, x, lax.rem(y + 6, 8))
    next_half = (lax.rem(seq + 4, 128), head)
    prev_half = (lax.rem(seq + 124, 128), head)
    up_x = at(z, lax.rem(x + 1, 4), y)
    down_x = at(z, lax.rem(x + 3, 4), y)
    up_z = at(lax.rem(z + 1, 4), x, y)
    down_z = at(lax.rem(z + 3, 4), x, y)
    next_line = (lax.rem(seq + 8, 128), head)
    prev_line = (lax.rem(seq + 120, 128), head)
    h_sib = zhi * 2 + 1 - core
    h_far = (1 - zhi) * 2 + core
    h_farsib = (1 - zhi) * 2 + 1 - core
    sib = (seq, h_sib)
    far = (seq, h_far)
    farsib = (seq, h_farsib)
    z_mid = lax.rem(z + 2, 4)
    seq_mid = (z_mid * 4 + x) * 8 + y
    zhi_up = lax.rem(zhi + lax.div(z + 2, 4), 2)
    h_up = zhi_up * 2 + core
    h_down = (1 - zhi_up) * 2 + core
    mid_up = (seq_mid, h_up)
    mid_down = (seq_mid, h_down)

    local = []

    def load(src, dst, pred=None):
        copy = pltpu.make_async_copy(src, dst, local_sem.at[len(local)])
        local.append(copy)
        if pred is None:
            copy.start()
        else:
            pl.when(pred)(lambda: copy.start())
        return copy

    def rows16(g, yy):
        return wbuf.at[pl.ds(pl.multiple_of(g * 128 + yy * 16, 16), 16), :]

    def rows128(g):
        return wbuf.at[pl.ds(pl.multiple_of(g * 128, 128), 128), :]

    def rows64(g, half):
        return wbuf.at[pl.ds(pl.multiple_of(g * 128 + half * 64, 64), 64), :]

    is_source = (z == 3) & (x == 3)
    first = [
        load(w_in, rows16(group, y)),
        load(k_in, kv.at[0, 8]),
        load(v_in, kv.at[1, 8]),
    ]
    source_loads = [
        load(k_in, lkv.at[0, y], is_source),
        load(v_in, lkv.at[1, y], is_source),
    ]
    later = [
        load(res_in, rest),
        load(q_in, q), load(oq_in, oq), load(ok_in, ok), load(ov_in, ov),
        load(ores_in, ores), load(gain_in, gain),
    ]

    barrier = pltpu.get_barrier_semaphore()
    partners = [
        up_y, down_y, up_x, down_x, up_z, down_z, next_line, prev_line,
        sib, far, farsib, mid_up, mid_down, at(z_mid, x, y),
        up_y2, down_y2, next_half, prev_half,
    ]
    for partner in partners:
        pl.semaphore_signal(barrier, inc=1, device_id=partner, device_id_type=MESH)
    for copy in first:
        copy.wait()

    @pl.when(is_source)
    def _():
        for copy in source_loads:
            copy.wait()

    pl.semaphore_wait(barrier, len(partners))

    sent = []
    n_sent = [0]
    received = {}

    def recv_id(name, count=1):
        if name not in received:
            received[name] = recv_id.next
            recv_id.next += count
            assert recv_id.next <= N_RECV
        return received[name]

    recv_id.next = 0

    def remote(src, dst, recv, device):
        n_sent[0] += 1
        assert n_sent[0] <= N_SEND
        return pltpu.make_async_remote_copy(
            src_ref=src, dst_ref=dst, send_sem=send_sem.at[n_sent[0] - 1],
            recv_sem=recv_sem.at[recv], device_id=device, device_id_type=MESH,
        )

    def send(src, dst, recv, device, pred=None):
        copy = remote(src, dst, recv, device)
        sent.append((copy, pred))
        if pred is None:
            copy.start()
        else:
            pl.when(pred)(lambda: copy.start())

    def arrived(ref, recv, pred=None):
        copy = pltpu.make_async_remote_copy(
            src_ref=ref, dst_ref=ref, send_sem=send_sem.at[0],
            recv_sem=recv_sem.at[recv], device_id=sib, device_id_type=MESH,
        )
        if pred is None:
            copy.wait_recv()
        else:
            pl.when(pred)(lambda: copy.wait_recv())

    def drain():
        for copy, pred in sent:
            if pred is None:
                copy.wait_send()
            else:
                pl.when(pred)(lambda copy=copy: copy.wait_send())
        sent.clear()

    def mod8(value):
        return lax.rem(value + 8, 8)

    zhalf = lax.div(z, 2)
    order = [
        z,
        z - 1 + 2 * (1 - lax.div(z + 3, 4)),
        2 + zhalf * (1 - 2 * lax.rem(z, 2)),
        3 * (1 - zhalf),
    ]
    wz = recv_id("wz", 4)
    xl = [recv_id(("xl", i)) for i in range(4)]
    xr = [recv_id(("xr", i)) for i in range(4)]
    hl = [recv_id(("hl", i)) for i in range(4)]
    hr = [recv_id(("hr", i)) for i in range(4)]

    def spread(piece):
        send(piece, piece, xl[0], up_x)
        send(piece, piece, xr[0], down_x)
        send(piece, piece, wz + z, up_z, z < 3)
        send(piece, piece, wz + z, down_z, z > 0)

    def wy_piece(d):
        return rows16(group, mod8(y - d))

    def wy_id(d):
        return recv_id(("wy", d))

    def wy_start():
        piece = wy_piece(0)
        send(piece, piece, wy_id(2), up_y2)
        send(piece, piece, wy_id(-2), down_y2)
        send(piece, piece, wy_id(1), up_y)
        send(piece, piece, wy_id(-1), down_y)
        spread(piece)

    def wy_take(d):
        piece = wy_piece(d)
        arrived(piece, wy_id(d))
        if d == 2:
            send(piece, piece, wy_id(3), up_y)
            send(piece, piece, wy_id(4), up_y2)
        if d == -2:
            send(piece, piece, wy_id(-3), down_y)
        spread(piece)

    inner = (z == 1) | (z == 2)

    def x_send(i):
        piece = rows128(order[i] * 4 + x)
        send(piece, piece, xl[i], up_x)
        send(piece, piece, xr[i], down_x)

    def z_take(i, pred=None):
        arrived(rows128(order[i] * 4 + x), wz + order[i], pred)

    def z_near():
        z_take(1)
        piece = rows128(order[1] * 4 + x)
        send(piece, piece, wz + order[1], up_z, (order[1] < z) & inner)
        x_send(1)
        z_take(2, inner)
        piece = rows128(order[2] * 4 + x)
        send(piece, piece, wz + order[2], down_z, (order[2] > z) & inner)

    def z_mid_event():
        z_take(2, (z == 0) | (z == 3))
        z_take(3, inner)
        piece = rows128(order[3] * 4 + x)
        send(piece, piece, wz + order[3], down_z, z == 1)
        send(piece, piece, wz + order[3], up_z, z == 2)
        x_send(2)

    def z_last():
        z_take(3, (z == 0) | (z == 3))
        x_send(3)

    def x_full(i):
        left = order[i] * 4 + lax.rem(x + 3, 4)
        right = order[i] * 4 + lax.rem(x + 1, 4)
        arrived(rows128(left), xl[i])
        send(rows64(left, 0), rows64(left, 0), hl[i], up_x)
        arrived(rows128(right), xr[i])
        send(rows64(right, 1), rows64(right, 1), hr[i], down_x)

    def x_half(i):
        across = order[i] * 4 + lax.rem(x + 2, 4)
        arrived(rows64(across, 0), hl[i])
        arrived(rows64(across, 1), hr[i])

    def kv_send(p, slot, to_slot, device, pred=None):
        send(kv.at[p, slot], kv.at[p, to_slot], recv_id(("kv", to_slot, p)), device, pred)

    def kv_wait(p, slot, pred=None):
        arrived(kv.at[p, slot], recv_id(("kv", slot, p)), pred)

    def kv_own(p):
        kv_send(p, 8, 7, up_y, y < 7)
        kv_send(p, 8, 4, next_half)
        kv_send(p, 8, 0, next_line)

    def kv_near(r, p):
        if r <= 3:
            m = r - 1
            kv_wait(p, m, y <= 7 - m)
            kv_send(p, m, m + 1, down_y, (y <= 7 - m) & (y > 0))
            kv_wait(p, 8 - r, y >= r)
            if r < 3:
                kv_send(p, 8 - r, 7 - r, up_y, (y >= r) & (y < 7))
        else:
            kv_wait(p, 3, y <= 4)

    def kv_far(r, p):
        if r == 1:
            kv_wait(p, 4)
            kv_send(p, 4, 3, up_y, (y >= 4) & (y < 7))
            kv_send(p, 4, 5, down_y, (y < 4) & (y > 0))
            return
        k = 3 + r
        kv_wait(p, 8 - k, y >= k)
        kv_wait(p, k, y <= 7 - k)
        if k < 7:
            kv_send(p, 8 - k, 7 - k, up_y, (y >= k) & (y < 7))
            kv_send(p, k, k + 1, down_y, (y <= 7 - k) & (y > 0))

    depth = lax.select(x == 3, 0, lax.select(x == 1, 2, 1)) + 3 - z
    tree_up = (z == 3) & ((x == 3) | (x == 0))
    tree_down = (z == 3) & (x == 3)
    tree_copies = []
    for p in range(2):
        piece = lkv.at[p, y]
        tree_id = recv_id(("tree", p))
        for device, pred in ((up_x, tree_up), (down_x, tree_down), (down_z, z > 0)):
            tree_copies.append((remote(piece, piece, tree_id, device), pred))
    sent.extend(tree_copies)

    def tree(k, p):
        here = depth == k
        if k:
            arrived(lkv.at[p, y], recv_id(("tree", p)), here)
        for copy, pred in tree_copies[3 * p:3 * p + 3]:
            pl.when(here & pred)(lambda copy=copy: copy.start())

    def l_up(k, p):
        last = 4 - p
        if k > last:
            return
        piece = lkv.at[p, mod8(y - k)]
        if k:
            arrived(piece, recv_id(("lp", k, p)))
        if k < last:
            send(piece, piece, recv_id(("lp", k + 1, p)), up_y)

    def l_down(k, p):
        last = 3 + p
        if k > last:
            return
        piece = lkv.at[p, lax.rem(y + k, 8)]
        if k:
            arrived(piece, recv_id(("lm", k, p)))
        if k < last:
            send(piece, piece, recv_id(("lm", k + 1, p)), down_y)

    def l_step(k):
        for p in range(2):
            l_up(k, p)
            l_down(k, p)

    def prefix_pair(i):
        keys = kv[0, :, :, i * HD:(i + 1) * HD].reshape(9 * TOK, HD)
        vals = kv[1, :, :, i * HD:(i + 1) * HD].reshape(9 * TOK, HD)
        for half in range(2):
            c = (2 * i + half) * HD
            scores = score_dot(q[:, c:c + HD], keys)
            row = lax.broadcasted_iota(jnp.int32, scores.shape, 0)
            col = lax.broadcasted_iota(jnp.int32, scores.shape, 1)
            allowed = (col > row) & (col <= row + WINDOW) & (col >= (8 - seq) * TOK)
            scores = jnp.where(allowed, scores, -jnp.inf)
            abuf[head, i, 0:TOK, half * HD:(half + 1) * HD] = softmax_dot(
                scores, vals
            ).astype(jnp.bfloat16)

    def option_pair(i):
        keys = lkv[0, :, :, i * HD:(i + 1) * HD].reshape(WINDOW, HD)
        vals = lkv[1, :, :, i * HD:(i + 1) * HD].reshape(WINDOW, HD)
        own_keys = ok[:, i * HD:(i + 1) * HD]
        own_vals = ov[:, i * HD:(i + 1) * HD]
        for half in range(2):
            c = (2 * i + half) * HD
            query = oq[:, c:c + HD]
            shared = score_dot(query, keys)
            own = score_dot(query, own_keys)
            row = lax.broadcasted_iota(jnp.int32, shared.shape, 0)
            col = lax.broadcasted_iota(jnp.int32, shared.shape, 1)
            shared = jnp.where(col > row, shared, -jnp.inf)
            row = lax.broadcasted_iota(jnp.int32, own.shape, 0)
            col = lax.broadcasted_iota(jnp.int32, own.shape, 1)
            own = jnp.where(col <= row, own, -jnp.inf)
            top = jnp.maximum(
                jnp.max(shared, axis=1, keepdims=True), jnp.max(own, axis=1, keepdims=True)
            )
            ws = jnp.exp2((shared - top) * exp2_scale)
            wo = jnp.exp2((own - top) * exp2_scale)
            total = jnp.sum(ws, axis=1, keepdims=True) + jnp.sum(wo, axis=1, keepdims=True)
            out = jnp.dot(ws.astype(jnp.bfloat16), vals, preferred_element_type=jnp.float32)
            out = out + jnp.dot(
                wo.astype(jnp.bfloat16), own_vals, preferred_element_type=jnp.float32
            )
            abuf[head, i, TOK:ROWS, half * HD:(half + 1) * HD] = (out / total).astype(
                jnp.bfloat16
            )

    def part_rows(part):
        return pl.ds(0, TOK) if part == 0 else pl.ds(TOK, OPT)

    def exchange_send(part, i):
        rows = part_rows(part)
        piece = abuf.at[head, i, rows, :]
        send(piece, relay.at[i, rows, :], recv_id(("mid", part, i)), (mid_up, mid_down)[i])
        send(piece, piece, recv_id(("sib", part, i)), sib)

    def exchange_relay(part, i):
        rows = part_rows(part)
        piece = relay.at[i, rows, :]
        arrived(piece, recv_id(("mid", part, i)))
        origin = (h_down, h_up)[i]
        send(
            piece, abuf.at[origin, i, rows, :], recv_id(("far", part, i)),
            (mid_up, mid_down)[i],
        )

    def exchange_forward(part, i):
        piece = abuf.at[h_far, i, part_rows(part), :]
        arrived(piece, recv_id(("far", part, i)))
        send(piece, piece, recv_id(("farsib", part, i)), sib)

    def exchange_rest(part, i):
        arrived(abuf.at[h_sib, i, part_rows(part), :], recv_id(("sib", part, i)))
        arrived(abuf.at[h_farsib, i, part_rows(part), :], recv_id(("farsib", part, i)))

    def project(i):
        plane = order[i]
        part = None
        for pair in range(2):
            rows = pl.ds(pl.multiple_of(plane * 512 + pair * 256, 256), 256)
            new = jnp.dot(
                abuf[plane, pair], wbuf[rows, :], preferred_element_type=jnp.float32
            )
            part = new if part is None else part + new
        if i == 0:
            proj[...] = part
        else:
            proj[...] += part

    wy_start()
    tree(0, 0)
    tree(0, 1)
    wy_take(2)
    wy_take(-2)
    kv_own(0)
    kv_own(1)
    wy_take(1)
    wy_take(-1)
    tree(1, 0)
    tree(1, 1)
    wy_take(3)
    wy_take(-3)
    wy_take(4)
    kv_near(1, 0)
    kv_near(1, 1)
    z_near()
    x_full(0)
    kv_far(1, 0)
    kv_far(1, 1)
    tree(2, 0)
    tree(2, 1)
    kv_near(2, 0)
    kv_near(2, 1)
    tree(3, 0)
    tree(3, 1)
    kv_far(2, 0)
    kv_far(2, 1)
    kv_near(3, 0)
    kv_near(3, 1)
    tree(4, 0)
    tree(4, 1)
    z_mid_event()
    x_full(1)
    kv_far(3, 0)
    kv_far(3, 1)
    tree(5, 0)
    tree(5, 1)
    kv_near(4, 0)
    kv_near(4, 1)
    later[0].wait()
    res[...] = rest[...].T
    kv_far(4, 0)
    kv_far(4, 1)
    l_step(0)
    for copy in later[1:5]:
        copy.wait()
    prefix_pair(0)
    exchange_send(0, 0)
    z_last()
    prefix_pair(1)
    exchange_send(0, 1)
    l_step(1)
    x_full(2)
    exchange_relay(0, 0)
    exchange_relay(0, 1)
    l_step(2)
    exchange_forward(0, 0)
    exchange_forward(0, 1)
    l_step(3)
    x_half(0)
    x_half(1)
    l_step(4)
    option_pair(0)
    exchange_send(1, 0)
    option_pair(1)
    exchange_send(1, 1)
    x_full(3)
    exchange_rest(0, 0)
    exchange_rest(0, 1)
    exchange_relay(1, 0)
    exchange_relay(1, 1)
    exchange_forward(1, 0)
    exchange_forward(1, 1)
    exchange_rest(1, 0)
    exchange_rest(1, 1)
    project(0)
    project(1)
    x_half(2)
    project(2)
    for copy in later[5:]:
        copy.wait()
    x_half(3)
    project(3)

    square = jnp.sum(proj[...] * proj[...], axis=1, keepdims=True)
    diag = (
        lax.broadcasted_iota(jnp.int32, (128, 128), 0)
        == lax.broadcasted_iota(jnp.int32, (128, 128), 1)
    )
    row0 = jnp.sum(jnp.where(diag, square[0:128], 0.0), axis=0, keepdims=True)
    row1 = jnp.sum(jnp.where(diag[0:64], square[128:192], 0.0), axis=0, keepdims=True)
    ssq[head] = jnp.concatenate([row0, row1, jnp.zeros((6, 128), jnp.float32)], axis=0)
    mine = ssq.at[head]
    send(mine, mine, recv_id("sq0"), far)
    send(mine, mine, recv_id("sq1"), farsib)
    send(mine, mine, recv_id("sq2"), sib)
    drain()
    arrived(ssq.at[h_sib], recv_id("sq2"))
    arrived(ssq.at[h_far], recv_id("sq0"))
    arrived(ssq.at[h_farsib], recv_id("sq1"))
    total = ssq[0] + ssq[1] + ssq[2] + ssq[3]
    col0 = jnp.sum(jnp.where(diag, total[0:1], 0.0), axis=1, keepdims=True)
    col1 = jnp.sum(jnp.where(diag[0:64], total[1:2], 0.0), axis=1, keepdims=True)
    inv0 = lax.rsqrt(col0 / D + epsilon)
    inv1 = lax.rsqrt(col1 / D + epsilon)
    scale = gain[...].reshape(1, COLS)
    pout[...] = (
        (res[...].astype(jnp.float32) + proj[0:TOK, :] * inv0 * scale).astype(jnp.bfloat16).T
    )
    full = ores[...].astype(jnp.float32) + proj[TOK:ROWS, :] * inv1 * scale
    start = bounds[0, 0]
    length = bounds[0, 1]
    pos = lax.broadcasted_iota(jnp.int32, (OPT, COLS), 0)
    inside = pos < length
    out = jnp.where(inside, full, 0.0).astype(jnp.bfloat16)
    oout[...] = out
    chosen = inside & (pos >= start)
    picked = jnp.where(chosen, out.astype(jnp.float32), 0.0)
    count = jnp.broadcast_to((length - start).astype(jnp.float32), (1, COLS))
    osum[...] = jnp.sum(picked, axis=0, keepdims=True) / count
    drain()


def fused(*args):
    bf, f32 = jnp.bfloat16, jnp.float32
    anywhere = pl.BlockSpec(memory_space=pl.ANY)
    vmem = pl.BlockSpec(memory_space=pltpu.VMEM)
    return pl.pallas_call(
        kernel,
        out_shape=(
            jax.ShapeDtypeStruct((COLS, TOK), bf),
            jax.ShapeDtypeStruct((OPT, COLS), bf),
            jax.ShapeDtypeStruct((1, COLS), f32),
        ),
        in_specs=[anywhere] * 10 + [pl.BlockSpec(memory_space=pltpu.SMEM)],
        out_specs=(vmem, vmem, vmem),
        scratch_shapes=[
            pltpu.VMEM((TOK, 512), bf),
            pltpu.VMEM((OPT, 512), bf),
            pltpu.VMEM((OPT, 256), bf),
            pltpu.VMEM((OPT, 256), bf),
            pltpu.VMEM((COLS, TOK), bf),
            pltpu.VMEM((TOK, COLS), bf),
            pltpu.VMEM((OPT, COLS), bf),
            pltpu.VMEM((COLS,), f32),
            pltpu.VMEM((2, 9, TOK, 256), bf),
            pltpu.VMEM((2, 8, TOK, 256), bf),
            pltpu.VMEM((2048, COLS), bf),
            pltpu.VMEM((4, 2, ROWS, 256), bf),
            pltpu.VMEM((2, ROWS, 256), bf),
            pltpu.VMEM((ROWS, COLS), f32),
            pltpu.VMEM((4, 8, 128), f32),
            pltpu.SemaphoreType.DMA((16,)),
            pltpu.SemaphoreType.DMA((N_SEND,)),
            pltpu.SemaphoreType.DMA((N_RECV,)),
        ],
        compiler_params=pltpu.CompilerParams(
            collective_id=0, has_side_effects=True, vmem_limit_bytes=60 * 1024 * 1024
        ),
    )(*args)


def body(
    queries, keys, values, prefix_resid, opt_queries, opt_keys, opt_values, opt_resid,
    out_weight, norm_gain, option_bounds,
):
    prefix_out, option_out, option_summary = fused(
        queries, keys, values, prefix_resid.T, opt_queries[0], opt_keys[0], opt_values[0],
        opt_resid[0], out_weight, norm_gain, option_bounds,
    )
    return prefix_out.T, option_out[None], option_summary[None, 0]


def solution(mesh):
    return jax.shard_map(
        body,
        mesh=mesh,
        in_specs=(
            P("seq", "head"),
            P("seq", "head"),
            P("seq", "head"),
            P("seq", "head"),
            P("seq", None, "head"),
            P("seq", None, "head"),
            P("seq", None, "head"),
            P("seq", None, "head"),
            P("seq", "head"),
            P("head"),
            P("seq", None),
        ),
        out_specs=(P("seq", "head"), P("seq", None, "head"), P("seq", "head")),
        check_vma=False,
    )
```

time: 106 us -> 94.8 us (0.89)
  the two profiles are of different devices: /device:TPU:59 before, /device:TPU:6 now
where the time goes in v2:
time: 94.8 us; the launch traced here: 94.6 us
  Pallas kernels  90.9 us (96%)
  local copies, waits for them, and re-layouts  3.06 us (3%)
    pallas_call x1, Pallas kernels, fused(): pl.pallas_call(kernel, out_shape=(jax.ShapeDtypeStruct((COLS, TOK), bf),...  90.9 us
    unnamed x7, local copies, waits for them, and re-layouts  3.06 us

profile of v2, /device:TPU:6, one launch (start us, length us, event | category | flops | bytes accessed | tf_op | source)
XLA Modules:
  0.0 94.6 jit_solution(10953136462871861293)
XLA Ops:
  0.6 90.9 %shard_map.130 = (bf16[1344,128]{1,0:T(8,128)(2,1)}, bf16[64,1344]{1,0:T(8,128)(2,1)}, f32[1,1344]{1,0:T(1,128)}) custom-call(bf16[128,512]{1,0:T(8,128)(2,1)} %q_in.1, bf16[128,256]{1,0:T(8,128)(2,1)} %k_in.1, bf16[128,256]{1,0:T(8,128)(2,1)} %v_in.1, bf16[1344,128]{1,0:T(8,128)(2,1)} %bitcast.7, bf16[64,512]{1,0:T(8,128)(2,1)} %bitcast.11, ...), custom_call_target="tpu_custom_call" | custom-call | tf_op jit(solution)/shard_map/pallas_call | solution.py:567
  91.5 0.0 copy-start
  91.6 1.8 %copy.17 = bf16[128,1344]{0,1:T(8,128)(2,1)} copy(bf16[128,1344]{0,1:T(8,128)(2,1)} %bitcast.8) | data formatting | bytes 688128
  93.3 0.0 copy-done
  93.3 0.0 copy-start.1
  93.3 0.7 copy.18
  94.0 0.0 copy-done.1
  94.0 0.6 copy.19
Async XLA Ops:
  91.5 1.8 %copy-start = (bf16[64,1344]{1,0:T(8,128)(2,1)S(1)}, bf16[64,1344]{1,0:T(8,128)(2,1)}, u32[]{:S(2)}) copy-start(bf16[64,1344]{1,0:T(8,128)(2,1)} %get-tuple-element.7) | copy-start | bytes 516100
  93.3 0.7 copy-start.1

commit v3 on v2

--- a/solution.py
+++ b/solution.py
@@ -59,8 +59,6 @@
     down_y = at(z, x, lax.rem(y + 7, 8))
     up_y2 = at(z, x, lax.rem(y + 2, 8))
     down_y2 = at(z, x, lax.rem(y + 6, 8))
-    next_half = (lax.rem(seq + 4, 128), head)
-    prev_half = (lax.rem(seq + 124, 128), head)
     up_x = at(z, lax.rem(x + 1, 4), y)
     down_x = at(z, lax.rem(x + 3, 4), y)
     up_z = at(lax.rem(z + 1, 4), x, y)
@@ -121,7 +119,7 @@
     partners = [
         up_y, down_y, up_x, down_x, up_z, down_z, next_line, prev_line,
         sib, far, farsib, mid_up, mid_down, at(z_mid, x, y),
-        up_y2, down_y2, next_half, prev_half,
+        up_y2, down_y2,
     ]
     for partner in partners:
         pl.semaphore_signal(barrier, inc=1, device_id=partner, device_id_type=MESH)
@@ -280,32 +278,50 @@
 
     def kv_own(p):
         kv_send(p, 8, 7, up_y, y < 7)
-        kv_send(p, 8, 4, next_half)
         kv_send(p, 8, 0, next_line)
-
-    def kv_near(r, p):
-        if r <= 3:
-            m = r - 1
-            kv_wait(p, m, y <= 7 - m)
-            kv_send(p, m, m + 1, down_y, (y <= 7 - m) & (y > 0))
+        kv_send(p, 8, 1, down_y, y == 0)
+        kv_send(p, 8, 2, down_y2, y == 1)
+
+    def kv_step(r, p):
+        m = r - 1
+        kv_wait(p, m, y <= 7 - m)
+        if r == 1:
+            kv_send(p, 0, 7, up_y, y == 7)
+            kv_send(p, 0, 6, up_y2, y == 6)
+        if r <= 4:
+            kv_send(p, m, r, down_y, (y <= 7 - m) & (y > 0))
             kv_wait(p, 8 - r, y >= r)
-            if r < 3:
+            if r < 4:
                 kv_send(p, 8 - r, 7 - r, up_y, (y >= r) & (y < 7))
+            else:
+                kv_send(p, 4, 3, up_y, y == 6)
         else:
-            kv_wait(p, 3, y <= 4)
-
-    def kv_far(r, p):
+            kv_send(p, 4, 5, down_y, y == 1)
+            kv_wait(p, 3, y == 7)
+
+    def kv_side(r, p):
         if r == 1:
-            kv_wait(p, 4)
-            kv_send(p, 4, 3, up_y, (y >= 4) & (y < 7))
-            kv_send(p, 4, 5, down_y, (y < 4) & (y > 0))
-            return
-        k = 3 + r
-        kv_wait(p, 8 - k, y >= k)
-        kv_wait(p, k, y <= 7 - k)
-        if k < 7:
-            kv_send(p, 8 - k, 7 - k, up_y, (y >= k) & (y < 7))
-            kv_send(p, k, k + 1, down_y, (y <= 7 - k) & (y > 0))
+            kv_wait(p, 1, y == 7)
+            kv_send(p, 1, 2, down_y, y == 7)
+            kv_wait(p, 2, y == 7)
+            kv_send(p, 2, 3, down_y, y == 7)
+        if r == 2:
+            kv_wait(p, 2, y == 6)
+            kv_send(p, 2, 3, down_y, y == 6)
+            kv_wait(p, 7, y == 0)
+            kv_send(p, 7, 6, up_y, y == 0)
+            kv_wait(p, 6, y == 0)
+            kv_send(p, 6, 5, up_y, y == 0)
+        if r == 3:
+            kv_wait(p, 3, y == 6)
+            kv_wait(p, 3, y == 5)
+            kv_wait(p, 6, y == 1)
+            kv_send(p, 6, 5, up_y, y == 1)
+            kv_wait(p, 5, y == 1)
+        if r == 4:
+            kv_wait(p, 5, y == 2)
+        if r == 5:
+            kv_wait(p, 5, y == 0)
 
     depth = lax.select(x == 3, 0, lax.select(x == 1, 2, 1)) + 3 - z
     tree_up = (z == 3) & ((x == 3) | (x == 0))
@@ -418,12 +434,16 @@
         arrived(piece, recv_id(("far", part, i)))
         send(piece, piece, recv_id(("farsib", part, i)), sib)
 
-    def exchange_rest(part, i):
-        arrived(abuf.at[h_sib, i, part_rows(part), :], recv_id(("sib", part, i)))
-        arrived(abuf.at[h_farsib, i, part_rows(part), :], recv_id(("farsib", part, i)))
+    def exchange_sib(part):
+        for i in range(2):
+            arrived(abuf.at[h_sib, i, part_rows(part), :], recv_id(("sib", part, i)))
+
+    def exchange_farsib(part):
+        for i in range(2):
+            arrived(abuf.at[h_farsib, i, part_rows(part), :], recv_id(("farsib", part, i)))
 
     def project(i):
-        plane = order[i]
+        plane = (head, h_sib, h_far, h_farsib)[i]
         part = None
         for pair in range(2):
             rows = pl.ds(pl.multiple_of(plane * 512 + pair * 256, 256), 256)
@@ -450,75 +470,79 @@
     wy_take(3)
     wy_take(-3)
     wy_take(4)
-    kv_near(1, 0)
-    kv_near(1, 1)
+    kv_step(1, 0)
+    kv_step(1, 1)
+    tree(2, 0)
+    tree(2, 1)
     z_near()
     x_full(0)
-    kv_far(1, 0)
-    kv_far(1, 1)
-    tree(2, 0)
-    tree(2, 1)
-    kv_near(2, 0)
-    kv_near(2, 1)
+    kv_side(1, 0)
+    kv_side(1, 1)
+    kv_step(2, 0)
+    kv_step(2, 1)
+    kv_side(2, 0)
+    kv_side(2, 1)
+    kv_step(3, 0)
+    kv_step(3, 1)
     tree(3, 0)
     tree(3, 1)
-    kv_far(2, 0)
-    kv_far(2, 1)
-    kv_near(3, 0)
-    kv_near(3, 1)
+    kv_side(3, 0)
+    kv_side(3, 1)
+    z_mid_event()
+    x_full(1)
     tree(4, 0)
     tree(4, 1)
-    z_mid_event()
-    x_full(1)
-    kv_far(3, 0)
-    kv_far(3, 1)
+    kv_step(4, 0)
+    kv_step(4, 1)
+    kv_side(4, 0)
+    kv_side(4, 1)
     tree(5, 0)
     tree(5, 1)
-    kv_near(4, 0)
-    kv_near(4, 1)
-    later[0].wait()
-    res[...] = rest[...].T
-    kv_far(4, 0)
-    kv_far(4, 1)
     l_step(0)
+    kv_step(5, 0)
+    kv_step(5, 1)
+    kv_side(5, 0)
+    kv_side(5, 1)
     for copy in later[1:5]:
         copy.wait()
     prefix_pair(0)
     exchange_send(0, 0)
-    z_last()
+    l_step(1)
     prefix_pair(1)
     exchange_send(0, 1)
-    l_step(1)
+    z_last()
+    l_step(2)
     x_full(2)
+    l_step(3)
     exchange_relay(0, 0)
+    x_half(0)
+    l_step(4)
     exchange_relay(0, 1)
-    l_step(2)
-    exchange_forward(0, 0)
-    exchange_forward(0, 1)
-    l_step(3)
-    x_half(0)
-    x_half(1)
-    l_step(4)
     option_pair(0)
     exchange_send(1, 0)
     option_pair(1)
     exchange_send(1, 1)
     x_full(3)
-    exchange_rest(0, 0)
-    exchange_rest(0, 1)
+    exchange_forward(0, 0)
+    exchange_forward(0, 1)
     exchange_relay(1, 0)
     exchange_relay(1, 1)
+    x_half(1)
+    later[0].wait()
+    res[...] = rest[...].T
     exchange_forward(1, 0)
     exchange_forward(1, 1)
-    exchange_rest(1, 0)
-    exchange_rest(1, 1)
-    project(0)
-    project(1)
     x_half(2)
-    project(2)
     for copy in later[5:]:
         copy.wait()
     x_half(3)
+    project(0)
+    exchange_sib(0)
+    exchange_sib(1)
+    project(1)
+    project(2)
+    exchange_farsib(0)
+    exchange_farsib(1)
     project(3)
 
     square = jnp.sum(proj[...] * proj[...], axis=1, keepdims=True)

time: 94.8 us -> 88.5 us (0.934)
  the two profiles are of different devices: /device:TPU:6 before, /device:TPU:3 now
where the time goes in v3:
time: 88.5 us; the launch traced here: 88.3 us
  Pallas kernels  84.6 us (96%)
  local copies, waits for them, and re-layouts  3.06 us (3%)
    pallas_call x1, Pallas kernels, fused(): pl.pallas_call(kernel, out_shape=(jax.ShapeDtypeStruct((COLS, TOK), bf),...  84.6 us
    unnamed x7, local copies, waits for them, and re-layouts  3.06 us

profile of v3, /device:TPU:3, one launch (start us, length us, event | category | flops | bytes accessed | tf_op | source)
XLA Modules:
  0.0 88.3 jit_solution(16868911079987502767)
XLA Ops:
  0.6 84.6 %shard_map.130 = (bf16[1344,128]{1,0:T(8,128)(2,1)}, bf16[64,1344]{1,0:T(8,128)(2,1)}, f32[1,1344]{1,0:T(1,128)}) custom-call(bf16[128,512]{1,0:T(8,128)(2,1)} %q_in.1, bf16[128,256]{1,0:T(8,128)(2,1)} %k_in.1, bf16[128,256]{1,0:T(8,128)(2,1)} %v_in.1, bf16[1344,128]{1,0:T(8,128)(2,1)} %bitcast.7, bf16[64,512]{1,0:T(8,128)(2,1)} %bitcast.11, ...), custom_call_target="tpu_custom_call" | custom-call | tf_op jit(solution)/shard_map/pallas_call | solution.py:591
  85.3 0.0 copy-start
  85.3 1.8 %copy.17 = bf16[128,1344]{0,1:T(8,128)(2,1)} copy(bf16[128,1344]{0,1:T(8,128)(2,1)} %bitcast.8) | data formatting | bytes 688128
  87.0 0.0 copy-done
  87.0 0.0 copy-start.1
  87.0 0.7 copy.18
  87.7 0.0 copy-done.1
  87.7 0.6 copy.19
Async XLA Ops:
  85.3 1.8 %copy-start = (bf16[64,1344]{1,0:T(8,128)(2,1)S(1)}, bf16[64,1344]{1,0:T(8,128)(2,1)}, u32[]{:S(2)}) copy-start(bf16[64,1344]{1,0:T(8,128)(2,1)} %get-tuple-element.7) | copy-start | bytes 516100
  87.0 0.7 copy-start.1

commit v4 on v3

--- a/solution.py
+++ b/solution.py
@@ -118,7 +118,7 @@
     barrier = pltpu.get_barrier_semaphore()
     partners = [
         up_y, down_y, up_x, down_x, up_z, down_z, next_line, prev_line,
-        sib, far, farsib, mid_up, mid_down, at(z_mid, x, y),
+        sib, far, farsib, mid_up, mid_down,
         up_y2, down_y2,
     ]
     for partner in partners:
@@ -474,6 +474,8 @@
     kv_step(1, 1)
     tree(2, 0)
     tree(2, 1)
+    later[0].wait()
+    res[...] = rest[...].T
     z_near()
     x_full(0)
     kv_side(1, 0)
@@ -528,8 +530,6 @@
     exchange_relay(1, 0)
     exchange_relay(1, 1)
     x_half(1)
-    later[0].wait()
-    res[...] = rest[...].T
     exchange_forward(1, 0)
     exchange_forward(1, 1)
     x_half(2)
@@ -586,7 +586,6 @@
 
 def fused(*args):
     bf, f32 = jnp.bfloat16, jnp.float32
-    anywhere = pl.BlockSpec(memory_space=pl.ANY)
     vmem = pl.BlockSpec(memory_space=pltpu.VMEM)
     return pl.pallas_call(
         kernel,
@@ -595,7 +594,8 @@
             jax.ShapeDtypeStruct((OPT, COLS), bf),
             jax.ShapeDtypeStruct((1, COLS), f32),
         ),
-        in_specs=[anywhere] * 10 + [pl.BlockSpec(memory_space=pltpu.SMEM)],
+        in_specs=[pl.BlockSpec(memory_space=pltpu.HBM)] * 10
+        + [pl.BlockSpec(memory_space=pltpu.SMEM)],
         out_specs=(vmem, vmem, vmem),
         scratch_shapes=[
             pltpu.VMEM((TOK, 512), bf),
@@ -623,6 +623,32 @@
     )(*args)
 
 
+def write_kernel(a_in, b_in, c_in, a_out, b_out, c_out, a, b, c, sems):
+    ways = [(a_in, a, a_out), (b_in, b, b_out), (c_in, c, c_out)]
+    reads = [pltpu.make_async_copy(w[0], w[1], sems.at[i]) for i, w in enumerate(ways)]
+    writes = [pltpu.make_async_copy(w[1], w[2], sems.at[3 + i]) for i, w in enumerate(ways)]
+    for read in reads:
+        read.start()
+    for read, write in zip(reads, writes):
+        read.wait()
+        write.start()
+    for write in writes:
+        write.wait()
+
+
+def written(*results):
+    hbm = pl.BlockSpec(memory_space=pltpu.HBM)
+    return pl.pallas_call(
+        write_kernel,
+        out_shape=tuple(jax.ShapeDtypeStruct(r.shape, r.dtype) for r in results),
+        in_specs=[hbm] * 3,
+        out_specs=(hbm,) * 3,
+        scratch_shapes=[pltpu.VMEM(r.shape, r.dtype) for r in results]
+        + [pltpu.SemaphoreType.DMA((6,))],
+        compiler_params=pltpu.CompilerParams(vmem_limit_bytes=60 * 1024 * 1024),
+    )(*results)
+
+
 def body(
     queries, keys, values, prefix_resid, opt_queries, opt_keys, opt_values, opt_resid,
     out_weight, norm_gain, option_bounds,
@@ -631,6 +657,7 @@
         queries, keys, values, prefix_resid.T, opt_queries[0], opt_keys[0], opt_values[0],
         opt_resid[0], out_weight, norm_gain, option_bounds,
     )
+    prefix_out, option_out, option_summary = written(prefix_out, option_out, option_summary)
     return prefix_out.T, option_out[None], option_summary[None, 0]
 
 

time: 88.5 us -> 87.2 us (0.985)
  local copies, waits for them, and re-layouts: 3.06 us -> 0 us
  Pallas kernels: 84.6 us -> 86.4 us
    unnamed x7 -> x0, local copies, waits for them, and re-layouts: 3.06 us -> none
    pallas_call x0 -> x1, Pallas kernels: none -> 1.82 us  [written(): pl.pallas_call(write_kernel, out_shape=tuple((jax.ShapeDtypeStruct(r.shap...]
where the time goes in v4:
time: 87.2 us; the launch traced here: 87.1 us
  Pallas kernels  86.4 us (99%)
    pallas_call x1, Pallas kernels, fused(): pl.pallas_call(kernel, out_shape=(jax.ShapeDtypeStruct((COLS, TOK), bf),...  84.6 us
    pallas_call x1, Pallas kernels, written(): pl.pallas_call(write_kernel, out_shape=tuple((jax.ShapeDtypeStruct(r.shap...  1.82 us

profile of v4, /device:TPU:3, one launch (start us, length us, event | category | flops | bytes accessed | tf_op | source)
XLA Modules:
  0.0 87.1 jit_solution(13046422756310552692)
XLA Ops:
  0.6 84.6 %shard_map.130 = (bf16[1344,128]{1,0:T(8,128)(2,1)}, bf16[64,1344]{1,0:T(8,128)(2,1)}, f32[1,1344]{1,0:T(1,128)}) custom-call(bf16[128,512]{1,0:T(8,128)(2,1)} %q_in.1, bf16[128,256]{1,0:T(8,128)(2,1)} %k_in.1, bf16[128,256]{1,0:T(8,128)(2,1)} %v_in.1, bf16[1344,128]{1,0:T(8,128)(2,1)} %bitcast.7, bf16[64,512]{1,0:T(8,128)(2,1)} %bitcast.9, ...), custom_call_target="tpu_custom_call" | custom-call | tf_op jit(solution)/shard_map/pallas_call | solution.py:590
  85.3 1.8 %shard_map.131 = (bf16[1344,128]{1,0:T(8,128)(2,1)}, bf16[64,1344]{1,0:T(8,128)(2,1)}, f32[1,1344]{1,0:T(1,128)}) custom-call(bf16[1344,128]{1,0:T(8,128)(2,1)} %get-tuple-element.9.a_in, bf16[64,1344]{1,0:T(8,128)(2,1)} %get-tuple-element.10.b_in, f32[1,1344]{1,0:T(1,128)} %get-tuple-element.11.c_in), custom_call_target="tpu_custom_call" | custom-call | tf_op jit(solution)/shard_map/pallas_call | solution.py:641

commit v5 on v4

--- a/solution.py
+++ b/solution.py
@@ -624,9 +624,12 @@
 
 
 def write_kernel(a_in, b_in, c_in, a_out, b_out, c_out, a, b, c, sems):
-    ways = [(a_in, a, a_out), (b_in, b, b_out), (c_in, c, c_out)]
+    piece = COLS // 4
+    parts = [pl.ds(i * piece, piece) for i in range(4)]
+    ways = [(a_in.at[r, :], a.at[r, :], a_out.at[r, :]) for r in parts]
+    ways += [(b_in, b, b_out), (c_in, c, c_out)]
     reads = [pltpu.make_async_copy(w[0], w[1], sems.at[i]) for i, w in enumerate(ways)]
-    writes = [pltpu.make_async_copy(w[1], w[2], sems.at[3 + i]) for i, w in enumerate(ways)]
+    writes = [pltpu.make_async_copy(w[1], w[2], sems.at[6 + i]) for i, w in enumerate(ways)]
     for read in reads:
         read.start()
     for read, write in zip(reads, writes):
@@ -644,7 +647,7 @@
         in_specs=[hbm] * 3,
         out_specs=(hbm,) * 3,
         scratch_shapes=[pltpu.VMEM(r.shape, r.dtype) for r in results]
-        + [pltpu.SemaphoreType.DMA((6,))],
+        + [pltpu.SemaphoreType.DMA((12,))],
         compiler_params=pltpu.CompilerParams(vmem_limit_bytes=60 * 1024 * 1024),
     )(*results)
 

time: 87.2 us -> 87.3 us (level)
  no operation moved by 1% of the time
where the time goes in v5:
time: 87.3 us; the launch traced here: 87.1 us
  Pallas kernels  86.5 us (99%)
    pallas_call x1, Pallas kernels, fused(): pl.pallas_call(kernel, out_shape=(jax.ShapeDtypeStruct((COLS, TOK), bf),...  84.6 us
    pallas_call x1, Pallas kernels, written(): pl.pallas_call(write_kernel, out_shape=tuple((jax.ShapeDtypeStruct(r.shap...  1.87 us

profile of v5, /device:TPU:3, one launch (start us, length us, event | category | flops | bytes accessed | tf_op | source)
XLA Modules:
  0.0 87.1 jit_solution(9641815719709167081)
XLA Ops:
  0.6 84.6 %shard_map.130 = (bf16[1344,128]{1,0:T(8,128)(2,1)}, bf16[64,1344]{1,0:T(8,128)(2,1)}, f32[1,1344]{1,0:T(1,128)}) custom-call(bf16[128,512]{1,0:T(8,128)(2,1)} %q_in.1, bf16[128,256]{1,0:T(8,128)(2,1)} %k_in.1, bf16[128,256]{1,0:T(8,128)(2,1)} %v_in.1, bf16[1344,128]{1,0:T(8,128)(2,1)} %bitcast.7, bf16[64,512]{1,0:T(8,128)(2,1)} %bitcast.9, ...), custom_call_target="tpu_custom_call" | custom-call | tf_op jit(solution)/shard_map/pallas_call | solution.py:590
  85.3 1.9 %shard_map.131 = (bf16[1344,128]{1,0:T(8,128)(2,1)}, bf16[64,1344]{1,0:T(8,128)(2,1)}, f32[1,1344]{1,0:T(1,128)}) custom-call(bf16[1344,128]{1,0:T(8,128)(2,1)} %get-tuple-element.9.a_in, bf16[64,1344]{1,0:T(8,128)(2,1)} %get-tuple-element.10.b_in, f32[1,1344]{1,0:T(1,128)} %get-tuple-element.11.c_in), custom_call_target="tpu_custom_call" | custom-call | tf_op jit(solution)/shard_map/pallas_call | solution.py:644
